TPU v7x, 32 devices: a whole 2x2x4 slice. The times are simulated.
32 devices in a mesh: rows: 8 (over z, y), mp: 4 (over x, core).
Axes of the slice: x: 2, y: 2, z: 4, core: 2. Of those that a mesh axis runs over, the one named last changes fastest.
Arguments:
- calib: bfloat16 [512, 8192], P('rows', 'mp'), may hold values from -40 to 40
- weight: bfloat16 [8192, 8192], P('rows', 'mp'), may hold values from -6 to 6
- inverse_factor: float32 [8192, 8192], P('rows', 'mp'), may hold values from -10 to 12, as said below
- pruned_blocks: int32 [7], replicated, may hold values from 0 to 63, as said below
Outputs:
- pruned_weight: bfloat16 [8192, 8192], P('rows', 'mp')
- next_gram: float32 [8192, 8192], P('rows', 'mp')
Inputs may be any that keep to these rules, and one draw needn't show every extreme that they name: `pruned_blocks`: 7 distinct block numbers in any order; block b holds rows b * 128 to b * 128 + 127. `inverse_factor`: symmetric and positive definite.
All inputs are finite; a program needn't handle non-finite values.
Results may differ from a plain program's by a relative error of at most 0.0095.
Values may be sent and summed in bfloat16 or wider, within the bound.
A program may use at most 128 MiB of HBM per device.

v0:
```python
import jax
import jax.numpy as jnp
from jax import lax
from jax.sharding import PartitionSpec as P

BLOCK = 128


def spd_solve(chol_lower, right_side):
    forward = lax.linalg.triangular_solve(chol_lower, right_side, left_side=True, lower=True)
    return lax.linalg.triangular_solve(
        chol_lower, forward, left_side=True, lower=True, transpose_a=True
    )


def shards(calib, weight, inverse_factor, pruned_blocks):
    rows_dev = weight.shape[0]
    width_dev = weight.shape[1]
    full_width = width_dev * lax.axis_size("mp")
    row_start = lax.axis_index("rows") * rows_dev
    col_start = lax.axis_index("mp") * width_dev
    starts = pruned_blocks * BLOCK
    block_count = pruned_blocks.shape[0]
    col_pieces = []
    for slot_index in range(block_count):
        offset = starts[slot_index] - col_start
        inside = ((offset >= 0) & (offset < width_dev)).astype(jnp.float32)
        clamped = jnp.clip(offset, 0, width_dev - BLOCK)
        col_pieces.append(lax.dynamic_slice_in_dim(inverse_factor, clamped, BLOCK, 1) * inside)
    columns = lax.psum(jnp.concatenate(col_pieces, axis=1), "mp")
    weight_parts = []
    inverse_parts = []
    for slot_index in range(block_count):
        offset = starts[slot_index] - row_start
        inside = ((offset >= 0) & (offset < rows_dev)).astype(jnp.float32)
        clamped = jnp.clip(offset, 0, rows_dev - BLOCK)
        weight_parts.append(
            lax.dynamic_slice_in_dim(weight, clamped, BLOCK, 0).astype(jnp.float32) * inside
        )
        inverse_parts.append(lax.dynamic_slice_in_dim(columns, clamped, BLOCK, 0) * inside)
    kept_rows = lax.psum(jnp.concatenate(weight_parts, axis=0).astype(jnp.bfloat16), "rows").astype(
        jnp.float32
    )
    inverse_square = lax.psum(jnp.concatenate(inverse_parts, axis=0), "rows")
    chol_lower = jnp.linalg.cholesky(inverse_square)
    factors = spd_solve(chol_lower, columns.T)
    update = lax.dot_general(
        factors, kept_rows, (((0,), (0,)), ((), ())), precision=lax.Precision.HIGHEST
    )
    block_ids = (row_start + jnp.arange(rows_dev, dtype=jnp.int32)) // BLOCK
    kept_mask = 1.0 - jnp.any(block_ids[:, None] == pruned_blocks[None, :], axis=1).astype(
        jnp.float32
    )
    pruned_weight = ((weight.astype(jnp.float32) - update) * kept_mask[:, None]).astype(
        jnp.bfloat16
    )
    out_scale = float(full_width) ** (-0.5)
    partial_value = lax.dot_general(
        lax.all_gather(calib, "rows", axis=0, tiled=True),
        pruned_weight,
        (((1,), (1,)), ((), ())),
        preferred_element_type=jnp.float32,
    )
    token_count = partial_value.shape[0]
    own_rows = (
        lax.psum_scatter(partial_value, "mp", scatter_dimension=0, tiled=True) * out_scale
    ).astype(jnp.bfloat16)
    gram_term = lax.dot_general(
        own_rows,
        lax.all_gather(own_rows, "rows", axis=1, tiled=True),
        (((0,), (0,)), ((), ())),
        preferred_element_type=jnp.float32,
    )
    gram_block = (
        lax.psum_scatter(
            gram_term.astype(jnp.bfloat16), "mp", scatter_dimension=1, tiled=True
        ).astype(jnp.float32)
        / token_count
    )
    return (pruned_weight, gram_block)


def solution(mesh):
    return jax.shard_map(
        shards,
        mesh=mesh,
        in_specs=(P("rows", "mp"), P("rows", "mp"), P("rows", "mp"), P()),
        out_specs=(P("rows", "mp"), P("rows", "mp")),
        check_vma=False,
    )
```

profile of v0, /device:TPU:0, one launch (start us, length us, event | category | flops | bytes accessed | tf_op | source)
XLA Modules:
  0.0 823.5 jit_solution(16125952968231039749)
XLA Ops:
  13.0 4.4 constant_dynamic-slice_fusion.1
  17.4 2.0 copy.22
  35.9 75.9 %all-reduce.5.cloned.1.call-done = f32[1024,896]{0,1:T(8,128)} async-done(((f32[1024,896]{0,1:T(8,128)}), f32[1024,896]{0,1:T(8,128)}) %all-reduce.5.cloned.1.call-update) | async-done | bytes 3670032 | tf_op jit(solution)/shard_map/psum | solution.py:30
  122.4 2.0 fusion.51
  124.4 2.0 fusion.52
  126.4 2.0 fusion.53
  128.4 2.2 fusion.54
  130.5 2.0 fusion.55
  132.5 2.0 fusion.56
  134.5 2.0 fusion.57
  137.3 116.8 %all-reduce.7.cloned.1.call-done = f32[896,896]{0,1:T(8,128)} async-done(((f32[896,896]{0,1:T(8,128)}), f32[896,896]{0,1:T(8,128)}) %all-reduce.7.cloned.1.call-update) | async-done | bytes 3211280 | tf_op jit(solution)/shard_map/psum | solution.py:44
  254.1 4.7 copy.21
  258.8 2.2 fusion
  262.7 11.7 %cholesky.195 = f32[128,128]{1,0:T(8,128)S(1)} custom-call(f32[128,128]{1,0:T(8,128)S(1)} %cholesky.502), custom_call_target="Cholesky" | custom-call | tf_op jit(solution)/shard_map/jit(cholesky)/cholesky | solution.py:45
  274.7 9.8 %custom-call.56 = f32[1,128,128]{1,2,0:T(8,128)S(1)} custom-call(f32[1,128,128]{2,1,0:T(8,128)S(1)} %get-tuple-element.55), custom_call_target="InvertDiagBlocksLowerTriangular" | custom-call | tf_op jit(solution)/shard_map/jit(cholesky)/cholesky | solution.py:45
  288.2 11.7 %cholesky.216 = f32[128,128]{1,0:T(8,128)S(1)} custom-call(f32[128,128]{1,0:T(8,128)S(1)} %cholesky.506), custom_call_target="Cholesky" | custom-call | tf_op jit(solution)/shard_map/jit(cholesky)/cholesky | solution.py:45
  301.3 10.2 %custom-call.57 = f32[1,128,128]{1,2,0:T(8,128)S(1)} custom-call(f32[1,128,128]{2,1,0:T(8,128)S(1)} %get-tuple-element.52), custom_call_target="InvertDiagBlocksLowerTriangular" | custom-call | tf_op jit(solution)/shard_map/jit(cholesky)/cholesky | solution.py:45
  315.2 13.2 %cholesky.411 = f32[128,128]{1,0:T(8,128)} custom-call(f32[128,128]{1,0:T(8,128)} %cholesky.511), custom_call_target="Cholesky" | custom-call | tf_op jit(solution)/shard_map/jit(cholesky)/cholesky | solution.py:45
  330.5 11.3 %custom-call.58 = f32[1,128,128]{1,2,0:T(8,128)} custom-call(f32[1,128,128]{2,1,0:T(8,128)} %get-tuple-element.49), custom_call_target="InvertDiagBlocksLowerTriangular" | custom-call | tf_op jit(solution)/shard_map/jit(cholesky)/cholesky | solution.py:45
  344.8 12.5 %cholesky.430 = f32[128,128]{1,0:T(8,128)} custom-call(f32[128,128]{1,0:T(8,128)S(1)} %cholesky.516), custom_call_target="Cholesky" | custom-call | tf_op jit(solution)/shard_map/jit(cholesky)/cholesky | solution.py:45
  358.9 10.4 %custom-call.59 = f32[1,128,128]{1,2,0:T(8,128)} custom-call(f32[1,128,128]{2,1,0:T(8,128)S(1)} %get-tuple-element.46), custom_call_target="InvertDiagBlocksLowerTriangular" | custom-call | tf_op jit(solution)/shard_map/jit(cholesky)/cholesky | solution.py:45
  372.2 11.7 %cholesky.449 = f32[128,128]{1,0:T(8,128)S(1)} custom-call(f32[128,128]{1,0:T(8,128)S(1)} %cholesky.521), custom_call_target="Cholesky" | custom-call | tf_op jit(solution)/shard_map/jit(cholesky)/cholesky | solution.py:45
  384.6 9.8 %custom-call.60 = f32[1,128,128]{1,2,0:T(8,128)S(1)} custom-call(f32[1,128,128]{2,1,0:T(8,128)S(1)} %get-tuple-element.43), custom_call_target="InvertDiagBlocksLowerTriangular" | custom-call | tf_op jit(solution)/shard_map/jit(cholesky)/cholesky | solution.py:45
  396.3 12.1 %cholesky.469 = f32[128,128]{1,0:T(8,128)S(1)} custom-call(f32[128,128]{1,0:T(8,128)S(1)} %cholesky.526), custom_call_target="Cholesky" | custom-call | tf_op jit(solution)/shard_map/jit(cholesky)/cholesky | solution.py:45
  409.1 9.8 %custom-call.61 = f32[1,128,128]{1,2,0:T(8,128)S(1)} custom-call(f32[1,128,128]{2,1,0:T(8,128)S(1)} %get-tuple-element.40), custom_call_target="InvertDiagBlocksLowerTriangular" | custom-call | tf_op jit(solution)/shard_map/jit(cholesky)/cholesky | solution.py:45
  420.4 11.7 %cholesky.487 = f32[128,128]{1,0:T(8,128)S(1)} custom-call(f32[128,128]{1,0:T(8,128)S(1)} %convolution_subtract_fusion.13), custom_call_target="Cholesky" | custom-call | tf_op jit(solution)/shard_map/jit(cholesky)/cholesky | solution.py:45
  437.3 1.9 select_select_fusion
  439.3 24.8 %while.1 = (s32[]{:T(128)}, f32[896,896]{1,0:T(8,128)}, s32[7,2]{0,1:T(2,128)S(1)}, f32[7,128,128]{2,1,0:T(8,128)}, s32[]{:T(128)}) while((s32[]{:T(128)}, f32[896,896]{1,0:T(8,128)}, s32[7,2]{0,1:T(2,128)S(1)}, f32[7,128,128]{2,1,0:T(8,128)}, s32[]{:T(128)}) %tuple.62), condition=%wide.while_cond, body=%wide.while_body.sunk | while | flops 2 | bytes 132705 | solution.py:11
  439.9 2.9 bitcast_dynamic-update-slice_fusion.2
  443.5 2.9 bitcast_dynamic-update-slice_fusion.2
  447.0 2.9 bitcast_dynamic-update-slice_fusion.2
  450.6 2.9 bitcast_dynamic-update-slice_fusion.2
  454.2 2.9 bitcast_dynamic-update-slice_fusion.2
  457.7 2.9 bitcast_dynamic-update-slice_fusion.2
  461.3 2.8 bitcast_dynamic-update-slice_fusion.2
  464.1 69.7 %custom-call.62 = f32[7,128,128]{1,2,0:T(8,128)S(1)} custom-call(f32[7,128,128]{2,1,0:T(8,128)} %get-tuple-element.9), custom_call_target="InvertDiagBlocksLowerTriangular" | custom-call | tf_op jit(solution)/shard_map/triangular_solve | solution.py:11
  533.9 1.9 constant_dynamic-update-slice_fusion.4
  538.1 1.9 convolution_subtract_fusion.1
  546.7 1.8 convolution_subtract_fusion.3
  558.9 1.9 convolution_subtract_fusion.2
  567.2 18.1 %multiply_convert_fusion = bf16[1024,2048]{1,0:T(8,128)(2,1)} fusion(bf16[1024,2048]{1,0:T(8,128)(2,1)} %param.5, f32[1024]{0:T(1024)S(1)} %convert_subtract_fusion, f32[896,1024]{1,0:T(8,128)} %constant_dynamic-update-slice_fusion.22, bf16[896,2048]{1,0:T(8,128)(2,1)} %all-reduce.9.cloned.1.call-done), kind=kOutput, calls=%fused_computation.4 | convolution fusion | flops 22556966912 | bytes 15732736 | tf_op jit(solution)/shard_map/dot_general | solution.py:47
  585.3 6.5 convolution_bitcast_fusion
  591.9 30.3 %reduce-scatter.3.cloned.1.call-done = f32[128,1024]{0,1:T(8,128)} async-done(((f32[512,1024]{0,1:T(8,128)}), f32[128,1024]{0,1:T(8,128)}) %reduce-scatter.3.cloned.1.call-update) | async-done | bytes 524304 | tf_op jit(solution)/shard_map/reduce_scatter | solution.py:66
  622.2 1.8 multiply_convert_fusion.8
  624.1 49.8 %all-gather.5.cloned.1.call-done = bf16[128,8192]{0,1:T(8,128)(2,1)} async-done(((bf16[128,1024]{0,1:T(8,128)(2,1)}), bf16[128,8192]{0,1:T(8,128)(2,1)}) %all-gather.5.cloned.1.call-update) | async-done | bytes 2097168 | tf_op jit(solution)/shard_map/all_gather | solution.py:70
  673.9 11.9 %convolution_convert_fusion = bf16[1024,8192]{1,0:T(8,128)(2,1)} fusion(bf16[128,1024]{0,1:T(8,128)(2,1)} %multiply_convert_fusion.8, bf16[128,8192]{0,1:T(8,128)(2,1)} %all-gather.5.cloned.1.call-done), kind=kOutput, calls=%fused_computation.2 | convolution fusion | flops 2155872256 | bytes 19136512 | tf_op jit(solution)/shard_map/dot_general | solution.py:68
  685.8 123.6 %reduce-scatter.5.cloned.1.call-done = bf16[1024,2048]{1,0:T(8,128)(2,1)} async-done(((bf16[1024,8192]{1,0:T(8,128)(2,1)}), bf16[1024,2048]{1,0:T(8,128)(2,1)}) %reduce-scatter.5.cloned.1.call-update) | async-done | bytes 4194320 | tf_op jit(solution)/shard_map/reduce_scatter | solution.py:75
  809.4 6.8 convert_multiply_fusion
  (155 shorter events, 80.7 us)
Async XLA Ops:
  7.2 104.6 %all-reduce.5.cloned.1.call-start = ((), (), s32[]{:S(2)}) async-start(), calls=%async_computation.2 | async-start | bytes 7340032 | tf_op jit(solution)/shard_map/psum | solution.py:30
  20.4 5.1 copy-start.5
  21.4 4.9 copy-start.6
  22.5 4.7 copy-start.7
  23.5 4.5 copy-start.8
  24.5 4.4 copy-start.9
  25.5 4.2 copy-start.10
  25.5 5.0 copy-start.11
  31.4 222.7 %all-reduce.7.cloned.1.call-start = ((), (), s32[]{:S(2)}) async-start(), calls=%async_computation.3 | async-start | bytes 6422528 | tf_op jit(solution)/shard_map/psum | solution.py:44
  120.6 1.7 copy-start.4
  122.3 444.9 %all-reduce.9.cloned.1.call-start = ((), (), s32[]{:S(2)}) async-start(), calls=%async_computation.4 | async-start | bytes 7340032 | tf_op jit(solution)/shard_map/psum | solution.py:41
  132.5 4.7 copy-start.13
  136.6 448.7 %all-gather.3.cloned.1.call-start = ((), (), s32[]{:S(2)}) async-start(), calls=%async_computation.5 | async-start | bytes 2359296 | tf_op jit(solution)/shard_map/all_gather | solution.py:59
  137.1 485.1 %reduce-scatter.3.cloned.1.call-start = ((), (), s32[]{:S(2)}) async-start(), calls=%async_computation.6 | async-start | bytes 2621440 | tf_op jit(solution)/shard_map/reduce_scatter | solution.py:66
  254.1 4.7 copy-start
  261.0 1.7 copy-start.3
  287.4 0.7 copy-start.12
  533.9 4.2 copy-start.1
  537.4 3.3 copy-start.2
  591.8 82.0 %all-gather.5.cloned.1.call-start = ((), (), s32[]{:S(2)}) async-start(), calls=%async_computation.7 | async-start | bytes 2359296 | tf_op jit(solution)/shard_map/all_gather | solution.py:70
  624.0 185.4 %reduce-scatter.5.cloned.1.call-start = ((), (), s32[]{:S(2)}) async-start(), calls=%async_computation.8 | async-start | bytes 20971520 | tf_op jit(solution)/shard_map/reduce_scatter | solution.py:75
Sparse Core Ops, SparseCore 0:
  31.5 80.1 all-reduce.4
  122.4 131.6 all-reduce.6
  258.3 141.9 all-reduce.8
  402.3 48.7 all-gather.2
  592.0 30.2 reduce-scatter.2
  624.8 49.0 all-gather.4
  686.0 123.4 reduce-scatter.4
where the time goes:
time: 830 us; the launch traced here: 824 us
  waiting for transfers between devices  397 us (48%)
  other arithmetic  265 us (32%)
  matrix products  79.4 us (10%)
  local copies, waits for them, and re-layouts  53 us (6%)
  between operations  28.5 us (3%)
    another operation x27, other arithmetic, shards(): chol_lower = jnp.linalg.cholesky(inverse_square)  153 us
    reduce_scatter x1, waiting for transfers between devices, shards(): lax.psum_scatter(gram_term.astype(jnp.bfloat16), 'mp', scatter_dimension=...  124 us
    psum x1, waiting for transfers between devices, shards(): inverse_square = lax.psum(jnp.concatenate(inverse_parts, axis=0), 'rows')  117 us
    psum x1, waiting for transfers between devices, shards(): columns = lax.psum(jnp.concatenate(col_pieces, axis=1), 'mp')  75.9 us
    another operation x3, other arithmetic, spd_solve(): lax.linalg.triangular_solve(chol_lower, forward, left_side=True, lower=Tr...  72.3 us
    all_gather x1, waiting for transfers between devices, shards(): lax.all_gather(own_rows, 'rows', axis=1, tiled=True)  49.8 us
    reduce_scatter x1, waiting for transfers between devices, shards(): lax.psum_scatter(partial_value, 'mp', scatter_dimension=0, tiled=True)  30.3 us
    another operation x21, local copies, waits for them, and re-layouts  24.8 us
  transfers between devices with their start and end apart: 7, of which 5 were waited for; matrix products, arithmetic and copies ran while one was open for 41% of the time, Pallas kernels for 0%

commit v1 on v0

--- a/solution.py
+++ b/solution.py
@@ -41,7 +41,7 @@
     kept_rows = lax.psum(jnp.concatenate(weight_parts, axis=0).astype(jnp.bfloat16), "rows").astype(
         jnp.float32
     )
-    inverse_square = lax.psum(jnp.concatenate(inverse_parts, axis=0), "rows")
+    inverse_square = jnp.sum(lax.all_gather(jnp.concatenate(inverse_parts, axis=0), "rows"), axis=0)
     chol_lower = jnp.linalg.cholesky(inverse_square)
     factors = spd_solve(chol_lower, columns.T)
     update = lax.dot_general(

time: 830 us -> 1230 us (1.48)
  waiting for transfers between devices: 397 us -> 758 us
  local copies, waits for them, and re-layouts: 53 us -> 78.5 us
    all_gather x0 -> x1, waiting for transfers between devices: none -> 476 us  [shards(): lax.all_gather(jnp.concatenate(inverse_parts, axis=0), 'rows')]
    psum x1 -> x0, waiting for transfers between devices: 117 us -> none  [shards(): inverse_square = lax.psum(jnp.concatenate(inverse_parts, axis=0), 'rows')]
    all_gather x0 -> x1, local copies, waits for them, and re-layouts: none -> 27.1 us  [shards(): lax.all_gather(jnp.concatenate(inverse_parts, axis=0), 'rows')]
  transfers between devices with their start and end apart: 7 -> 7, of which waited for: 5 -> 5; matrix products, arithmetic and copies ran while one was open for 41% -> 31% of each run, Pallas kernels for 0% -> 0%
where the time goes in v1:
time: 1230 us; the launch traced here: 1220 us
  waiting for transfers between devices  758 us (62%)
  other arithmetic  277 us (23%)
  matrix products  79.4 us (6%)
  local copies, waits for them, and re-layouts  78.5 us (6%)
  between operations  28 us (2%)
    all_gather x1, waiting for transfers between devices, shards(): lax.all_gather(jnp.concatenate(inverse_parts, axis=0), 'rows')  476 us
    another operation x27, other arithmetic, shards(): chol_lower = jnp.linalg.cholesky(inverse_square)  153 us
    reduce_scatter x1, waiting for transfers between devices, shards(): lax.psum_scatter(gram_term.astype(jnp.bfloat16), 'mp', scatter_dimension=...  124 us
    psum x1, waiting for transfers between devices, shards(): columns = lax.psum(jnp.concatenate(col_pieces, axis=1), 'mp')  75.9 us
    another operation x3, other arithmetic, spd_solve(): lax.linalg.triangular_solve(chol_lower, forward, left_side=True, lower=Tr...  72.3 us
    all_gather x1, waiting for transfers between devices, shards(): lax.all_gather(own_rows, 'rows', axis=1, tiled=True)  49.8 us
    reduce_scatter x1, waiting for transfers between devices, shards(): lax.psum_scatter(partial_value, 'mp', scatter_dimension=0, tiled=True)  31.6 us
    all_gather x1, local copies, waits for them, and re-layouts, shards(): lax.all_gather(jnp.concatenate(inverse_parts, axis=0), 'rows')  27.1 us
  transfers between devices with their start and end apart: 7, of which 5 were waited for; matrix products, arithmetic and copies ran while one was open for 31% of the time, Pallas kernels for 0%

profile of v1, /device:TPU:0, one launch (start us, length us, event | category | flops | bytes accessed | tf_op | source)
XLA Modules:
  0.0 1220.5 jit_solution(3139701847563368533)
XLA Ops:
  12.8 4.4 constant_dynamic-slice_fusion.1
  17.2 2.0 copy.18
  35.5 75.9 %all-reduce.4.cloned.1.call-done = f32[1024,896]{0,1:T(8,128)} async-done(((f32[1024,896]{0,1:T(8,128)}), f32[1024,896]{0,1:T(8,128)}) %all-reduce.4.cloned.1.call-update) | async-done | bytes 3670032 | tf_op jit(solution)/shard_map/psum | solution.py:30
  122.0 2.0 fusion.51
  124.1 2.0 fusion.52
  126.0 2.0 fusion.53
  128.0 2.1 fusion.54
  130.1 2.0 fusion.55
  132.2 2.1 fusion.56
  134.2 2.0 fusion.57
  137.0 476.1 %all-gather.9.cloned.1.call-done = f32[7168,896]{0,1:T(8,128)} async-done(((f32[896,896]{0,1:T(8,128)}), f32[7168,896]{0,1:T(8,128)}) %all-gather.9.cloned.1.call-update) | async-done | bytes 25690128 | tf_op jit(solution)/shard_map/all_gather | solution.py:44
  613.1 27.1 %copy.17 = f32[7168,896]{1,0:T(8,128)} copy(f32[7168,896]{0,1:T(8,128)} %all-gather.9.cloned.1.call-done) | data formatting | bytes 51380224 | tf_op jit(solution)/shard_map/all_gather | solution.py:44
  640.2 11.6 reduce_sum.9
  651.9 3.2 copy.16
  655.0 2.2 fusion
  659.0 11.7 cholesky.195
  670.9 9.8 custom-call.56
  684.4 11.7 cholesky.216
  697.5 10.2 custom-call.57
  711.4 13.2 %cholesky.411 = f32[128,128]{1,0:T(8,128)} custom-call(f32[128,128]{1,0:T(8,128)} %cholesky.511), custom_call_target="Cholesky" | custom-call | tf_op jit(solution)/shard_map/jit(cholesky)/cholesky | solution.py:45
  726.7 11.3 custom-call.58
  740.9 12.5 %cholesky.430 = f32[128,128]{1,0:T(8,128)} custom-call(f32[128,128]{1,0:T(8,128)S(1)} %cholesky.516), custom_call_target="Cholesky" | custom-call | tf_op jit(solution)/shard_map/jit(cholesky)/cholesky | solution.py:45
  755.0 10.4 custom-call.59
  768.3 11.7 cholesky.449
  780.7 9.8 custom-call.60
  792.4 12.1 cholesky.469
  805.1 9.8 custom-call.61
  816.5 11.7 cholesky.487
  833.1 1.9 select_select_fusion
  835.0 24.7 %while.1 = (s32[]{:T(128)}, f32[896,896]{1,0:T(8,128)}, s32[7,2]{0,1:T(2,128)S(1)}, f32[7,128,128]{2,1,0:T(8,128)}, s32[]{:T(128)}) while((s32[]{:T(128)}, f32[896,896]{1,0:T(8,128)}, s32[7,2]{0,1:T(2,128)S(1)}, f32[7,128,128]{2,1,0:T(8,128)}, s32[]{:T(128)}) %tuple.62), condition=%wide.while_cond, body=%wide.while_body.sunk | while | flops 2 | bytes 132705 | solution.py:11
  835.7 2.9 bitcast_dynamic-update-slice_fusion.2
  839.3 2.9 bitcast_dynamic-update-slice_fusion.2
  842.8 2.9 bitcast_dynamic-update-slice_fusion.2
  846.4 2.9 bitcast_dynamic-update-slice_fusion.2
  849.9 2.9 bitcast_dynamic-update-slice_fusion.2
  853.4 2.9 bitcast_dynamic-update-slice_fusion.2
  857.0 2.8 bitcast_dynamic-update-slice_fusion.2
  859.8 69.7 %custom-call.62 = f32[7,128,128]{1,2,0:T(8,128)S(1)} custom-call(f32[7,128,128]{2,1,0:T(8,128)} %get-tuple-element.9), custom_call_target="InvertDiagBlocksLowerTriangular" | custom-call | tf_op jit(solution)/shard_map/triangular_solve | solution.py:11
  929.5 1.9 constant_dynamic-update-slice_fusion.4
  933.8 1.9 convolution_subtract_fusion.1
  954.6 1.9 convolution_subtract_fusion.2
  962.9 18.1 %multiply_convert_fusion = bf16[1024,2048]{1,0:T(8,128)(2,1)} fusion(bf16[1024,2048]{1,0:T(8,128)(2,1)} %param.5, f32[1024]{0:T(1024)S(1)} %convert_subtract_fusion, f32[896,1024]{1,0:T(8,128)} %constant_dynamic-update-slice_fusion.22, bf16[896,2048]{1,0:T(8,128)(2,1)} %all-reduce.6.cloned.1.call-done), kind=kOutput, calls=%fused_computation.4 | convolution fusion | flops 22556966912 | bytes 15732736 | tf_op jit(solution)/shard_map/dot_general | solution.py:47
  981.0 6.5 convolution_bitcast_fusion
  987.6 31.6 %reduce-scatter.3.cloned.1.call-done = f32[128,1024]{0,1:T(8,128)} async-done(((f32[512,1024]{0,1:T(8,128)}), f32[128,1024]{0,1:T(8,128)}) %reduce-scatter.3.cloned.1.call-update) | async-done | bytes 524304 | tf_op jit(solution)/shard_map/reduce_scatter | solution.py:66
  1021.0 49.8 %all-gather.7.cloned.1.call-done = bf16[128,8192]{0,1:T(8,128)(2,1)} async-done(((bf16[128,1024]{0,1:T(8,128)(2,1)}), bf16[128,8192]{0,1:T(8,128)(2,1)}) %all-gather.7.cloned.1.call-update) | async-done | bytes 2097168 | tf_op jit(solution)/shard_map/all_gather | solution.py:70
  1070.9 11.9 convolution_convert_fusion
  1082.8 123.6 %reduce-scatter.5.cloned.1.call-done = bf16[1024,2048]{1,0:T(8,128)(2,1)} async-done(((bf16[1024,8192]{1,0:T(8,128)(2,1)}), bf16[1024,2048]{1,0:T(8,128)(2,1)}) %reduce-scatter.5.cloned.1.call-update) | async-done | bytes 4194320 | tf_op jit(solution)/shard_map/reduce_scatter | solution.py:75
  1206.4 6.8 convert_multiply_fusion
  (155 shorter events, 84.2 us)
Async XLA Ops:
  7.2 104.3 %all-reduce.4.cloned.1.call-start = ((), (), s32[]{:S(2)}) async-start(), calls=%async_computation.2 | async-start | bytes 7340032 | tf_op jit(solution)/shard_map/psum | solution.py:30
  20.2 5.1 copy-start.4
  21.2 4.9 copy-start.5
  22.3 4.7 copy-start.6
  23.3 4.5 copy-start.7
  24.3 4.4 copy-start.8
  25.3 4.2 copy-start.9
  25.3 5.0 copy-start.10
  31.2 581.9 %all-gather.9.cloned.1.call-start = ((), (), s32[]{:S(2)}) async-start(), calls=%async_computation.8 | async-start | bytes 28901376 | tf_op jit(solution)/shard_map/all_gather | solution.py:44
  120.3 1.7 copy-start.3
  122.0 840.9 %all-reduce.6.cloned.1.call-start = ((), (), s32[]{:S(2)}) async-start(), calls=%async_computation.3 | async-start | bytes 7340032 | tf_op jit(solution)/shard_map/psum | solution.py:41
  132.2 4.7 copy-start.12
  136.2 844.7 %all-gather.5.cloned.1.call-start = ((), (), s32[]{:S(2)}) async-start(), calls=%async_computation.4 | async-start | bytes 2359296 | tf_op jit(solution)/shard_map/all_gather | solution.py:59
  136.8 882.4 %reduce-scatter.3.cloned.1.call-start = ((), (), s32[]{:S(2)}) async-start(), calls=%async_computation.5 | async-start | bytes 2621440 | tf_op jit(solution)/shard_map/reduce_scatter | solution.py:66
  657.3 1.7 copy-start.2
  683.7 0.7 copy-start.11
  929.5 4.2 copy-start
  933.1 3.3 copy-start.1
  987.5 83.3 %all-gather.7.cloned.1.call-start = ((), (), s32[]{:S(2)}) async-start(), calls=%async_computation.6 | async-start | bytes 2359296 | tf_op jit(solution)/shard_map/all_gather | solution.py:70
  1021.0 185.4 %reduce-scatter.5.cloned.1.call-start = ((), (), s32[]{:S(2)}) async-start(), calls=%async_computation.7 | async-start | bytes 20971520 | tf_op jit(solution)/shard_map/reduce_scatter | solution.py:75
Sparse Core Ops, SparseCore 0:
  31.3 80.0 all-reduce.3
  122.1 490.9 all-gather.8
  617.4 142.9 all-reduce.5
  762.3 48.9 all-gather.4
  987.6 31.4 reduce-scatter.2
  1021.7 49.0 all-gather.6
  1082.9 123.4 reduce-scatter.4
